TPU v7x, 32 devices: a whole 2x2x4 slice. The times are simulated.
32 devices in a mesh: dp: 8 (over z, core), tensor: 4 (over y, x).
Axes of the slice: x: 2, y: 2, z: 4, core: 2. Of those that a mesh axis runs over, the one named last changes fastest.
Arguments:
- tokens: bfloat16 [4096, 2304], P(('dp', 'tensor')), may hold values from -6 to 6
- cotangent: bfloat16 [4096, 2304], P(('dp', 'tensor')), may hold values from -6 to 6
- doc_lengths: int32 [8, 4], P('dp'), may hold values from 0 to 512, as said below
- w_query: bfloat16 [2304, 2048], P('dp', 'tensor')
- w_key: bfloat16 [2304, 1024], P('dp')
- w_value: bfloat16 [2304, 1024], P('dp'), may hold values from -0.125 to 0.125
- w_out: bfloat16 [2048, 2304], P('tensor', 'dp'), may hold values from -0.125 to 0.125
- w_gate: bfloat16 [2304, 9216], P('dp', 'tensor'), may hold values from -0.125 to 0.125
- w_up: bfloat16 [2304, 9216], P('dp', 'tensor'), may hold values from -0.125 to 0.125
- w_down: bfloat16 [9216, 2304], P('tensor', 'dp'), may hold values from -0.0625 to 0.0625
- norm_gains: bfloat16 [4, 2304], P(None, 'dp'), may hold values from 0.099609375 to 1.8984375
Outputs:
- result: float32 [4096, 2304], P(('dp', 'tensor'))
- grad_tokens: float32 [4096, 2304], P(('dp', 'tensor'))
- grad_query: float32 [2304, 2048], P('dp', 'tensor')
- grad_key: float32 [2304, 1024], P('dp')
- grad_value: float32 [2304, 1024], P('dp')
- grad_out: float32 [2048, 2304], P('tensor', 'dp')
- grad_gate: float32 [2304, 9216], P('dp', 'tensor')
- grad_up: float32 [2304, 9216], P('dp', 'tensor')
- grad_down: float32 [9216, 2304], P('tensor', 'dp')
- grad_gains: float32 [4, 2304], P(None, 'dp')
Inputs may be any that keep to these rules, and one draw needn't show every extreme that they name: `doc_lengths`: each row lists the lengths of the documents packed in order from the first token slot of one dp index; a length may be 0; a row sums to between 256 and 512, some row sums to exactly 512, and some document has exactly 512 tokens.
All inputs are finite; a program needn't handle non-finite values.
Results may differ from a plain program's by a relative error of at most 0.015.
The roundings to bfloat16 on the way count: a program that leaves them out, or rounds other values in their place, can miss the bound.
Values may be sent and summed in bfloat16 or wider, within the bound.
No kernel may reach another device: no remote copies, remote signals or barrier semaphores. Data moves between devices by JAX's collectives and lax.ppermute only.
A program may use at most 192 MiB of HBM per device.

v0:
```python
import jax
import jax.numpy as jnp
from jax import lax
from jax.sharding import PartitionSpec as P

HQ = 8
KVH = 4
HD = 256


EPSILON = 1e-06
SOFT_CAP = 50.0


def inv_root(source):
    return lax.rsqrt(jnp.mean(source * source, axis=-1, keepdims=True) + EPSILON)


def norm_back(source, inverse, gain_row, upstream):
    unit_rows = source * inverse
    scaled = upstream * gain_row
    grad_input = inverse * (
        scaled - unit_rows * jnp.mean(scaled * unit_rows, axis=-1, keepdims=True)
    )
    return (grad_input, jnp.sum(upstream * unit_rows, axis=0))


def gated_unit(gate_in, up_in):
    return jax.nn.gelu(gate_in, approximate=True) * up_in


def shards(
    tokens, cotangent, doc_lengths, w_query, w_key, w_value, w_out, w_gate, w_up, w_down, norm_gains
):
    tensor_count = lax.axis_size("tensor")
    tensor_index = lax.axis_index("tensor")
    row_count = tokens.shape[0]
    group_size = row_count * tensor_count
    local_heads = w_query.shape[1] // HD
    local_kv = max(1, local_heads * KVH // HQ)
    copies = local_heads // local_kv
    kv_first = tensor_index * (local_heads * KVH) // HQ
    key_part = lax.dynamic_slice_in_dim(w_key, kv_first * HD, local_kv * HD, 1)
    value_part = lax.dynamic_slice_in_dim(w_value, kv_first * HD, local_kv * HD, 1)
    gathered = (
        lax.all_gather(w_query, "dp", axis=0, tiled=True),
        lax.all_gather(key_part, "dp", axis=0, tiled=True),
        lax.all_gather(value_part, "dp", axis=0, tiled=True),
        lax.all_gather(w_out, "dp", axis=1, tiled=True),
        lax.all_gather(w_gate, "dp", axis=0, tiled=True),
        lax.all_gather(w_up, "dp", axis=0, tiled=True),
        lax.all_gather(w_down, "dp", axis=1, tiled=True),
        lax.all_gather(norm_gains, "dp", axis=1, tiled=True),
    )
    (
        query_weight,
        key_weight,
        value_weight,
        out_weight,
        gate_weight,
        up_weight,
        down_weight,
        gain_table,
    ) = gathered
    norm_scale = gain_table.astype(jnp.float32)
    doc_ends = jnp.cumsum(doc_lengths[0])
    places = jnp.arange(group_size, dtype=jnp.int32)
    inside = jnp.sum((doc_ends[None, :] <= places[:, None]).astype(jnp.int32), axis=1)
    segment = jnp.where(places >= doc_ends[-1], doc_lengths.shape[1] + places, inside)
    block_count = max(1, group_size // 512)
    block_rows = group_size // block_count
    qk_scale = HD ** (-0.5)

    def block_scores(first_row, query_all, key_copies):
        query_block = query_all[first_row : first_row + block_rows]
        raw_scores = jnp.einsum(
            "qhd,khd->hqk", query_block, key_copies, preferred_element_type=jnp.float32
        )
        bent_scores = jnp.tanh(raw_scores * (qk_scale / SOFT_CAP))
        row_segment = segment[first_row : first_row + block_rows]
        row_places = places[first_row : first_row + block_rows]
        allowed = (row_segment[:, None] == segment[None, :]) & (
            places[None, :] <= row_places[:, None]
        )
        return (query_block, bent_scores, allowed)

    stream = tokens.astype(jnp.float32)
    scale_in = inv_root(stream)
    normed_attn = (stream * scale_in * norm_scale[0]).astype(jnp.bfloat16)
    attn_gathered = lax.all_gather(normed_attn, "tensor", axis=0, tiled=True)
    model_width = attn_gathered.shape[1]
    query_all = (
        jnp.dot(attn_gathered, query_weight, preferred_element_type=jnp.float32)
        .astype(jnp.bfloat16)
        .reshape(group_size, local_heads, HD)
    )
    key_heads = (
        jnp.dot(attn_gathered, key_weight, preferred_element_type=jnp.float32)
        .astype(jnp.bfloat16)
        .reshape(group_size, local_kv, HD)
    )
    value_heads = (
        jnp.dot(attn_gathered, value_weight, preferred_element_type=jnp.float32)
        .astype(jnp.bfloat16)
        .reshape(group_size, local_kv, HD)
    )
    key_copies = jnp.repeat(key_heads, copies, axis=1)
    value_copies = jnp.repeat(value_heads, copies, axis=1)
    head_outs = []
    log_totals = []
    for block_number in range(block_count):
        first_row = block_number * block_rows
        query_block, bent_scores, allowed = block_scores(first_row, query_all, key_copies)
        exp_scores = jnp.where(allowed[None], jnp.exp(SOFT_CAP * bent_scores), 0.0)
        row_total = jnp.sum(exp_scores, axis=-1, keepdims=True)
        prob_rows = (exp_scores / row_total).astype(jnp.bfloat16)
        head_outs.append(
            jnp.einsum("hqk,khd->qhd", prob_rows, value_copies, preferred_element_type=jnp.float32)
        )
        log_totals.append(jnp.log(row_total))
    attended = (
        jnp.concatenate(head_outs, axis=0)
        .astype(jnp.bfloat16)
        .reshape(group_size, local_heads * HD)
    )
    attn_mixed = lax.psum_scatter(
        jnp.dot(attended, out_weight, preferred_element_type=jnp.float32),
        "tensor",
        scatter_dimension=0,
        tiled=True,
    )
    scale_mix = inv_root(attn_mixed)
    middle = stream + attn_mixed * scale_mix * norm_scale[1]
    scale_mid = inv_root(middle)
    normed_ffn = (middle * scale_mid * norm_scale[2]).astype(jnp.bfloat16)
    ffn_gathered = lax.all_gather(normed_ffn, "tensor", axis=0, tiled=True)
    gate_out = jnp.dot(ffn_gathered, gate_weight, preferred_element_type=jnp.float32)
    up_out = jnp.dot(ffn_gathered, up_weight, preferred_element_type=jnp.float32)
    hidden = gated_unit(gate_out, up_out).astype(jnp.bfloat16)
    branch = lax.psum_scatter(
        jnp.dot(hidden, down_weight, preferred_element_type=jnp.float32),
        "tensor",
        scatter_dimension=0,
        tiled=True,
    )
    scale_ffn = inv_root(branch)
    result = middle + branch * scale_ffn * norm_scale[3]
    upstream = cotangent.astype(jnp.float32)
    grad_branch, gain_last = norm_back(branch, scale_ffn, norm_scale[3], upstream)
    branch_grads = lax.all_gather(grad_branch.astype(jnp.bfloat16), "tensor", axis=0, tiled=True)
    gathered = (
        lax.all_gather(w_query, "dp", axis=0, tiled=True),
        lax.all_gather(key_part, "dp", axis=0, tiled=True),
        lax.all_gather(value_part, "dp", axis=0, tiled=True),
        lax.all_gather(w_out, "dp", axis=1, tiled=True),
        lax.all_gather(w_gate, "dp", axis=0, tiled=True),
        lax.all_gather(w_up, "dp", axis=0, tiled=True),
        lax.all_gather(w_down, "dp", axis=1, tiled=True),
        lax.all_gather(norm_gains, "dp", axis=1, tiled=True),
    )
    (
        query_weight,
        key_weight,
        value_weight,
        out_weight,
        gate_weight,
        up_weight,
        down_weight,
        gain_table,
    ) = gathered
    norm_scale = gain_table.astype(jnp.float32)
    grad_down = jnp.dot(hidden.T, branch_grads, preferred_element_type=jnp.float32)
    grad_hidden = jnp.dot(branch_grads, down_weight.T, preferred_element_type=jnp.float32)
    unused_value, pullback = jax.vjp(gated_unit, gate_out, up_out)
    grad_gate_out, grad_up_out = pullback(grad_hidden)
    grad_gate_out = grad_gate_out.astype(jnp.bfloat16)
    grad_up_out = grad_up_out.astype(jnp.bfloat16)
    grad_w_gate = jnp.dot(ffn_gathered.T, grad_gate_out, preferred_element_type=jnp.float32)
    grad_w_up = jnp.dot(ffn_gathered.T, grad_up_out, preferred_element_type=jnp.float32)
    grad_normed_ffn = lax.psum_scatter(
        jnp.dot(grad_gate_out, gate_weight.T, preferred_element_type=jnp.float32)
        + jnp.dot(grad_up_out, up_weight.T, preferred_element_type=jnp.float32),
        "tensor",
        scatter_dimension=0,
        tiled=True,
    )
    grad_mid_norm, gain_third = norm_back(middle, scale_mid, norm_scale[2], grad_normed_ffn)
    grad_middle = upstream + grad_mid_norm
    grad_mixed, gain_second = norm_back(attn_mixed, scale_mix, norm_scale[1], grad_middle)
    mixed_grads = lax.all_gather(grad_mixed.astype(jnp.bfloat16), "tensor", axis=0, tiled=True)
    grad_w_out = jnp.dot(attended.T, mixed_grads, preferred_element_type=jnp.float32)
    grad_attended = (
        jnp.dot(mixed_grads, out_weight.T, preferred_element_type=jnp.float32)
        .astype(jnp.bfloat16)
        .reshape(group_size, local_heads, HD)
    )
    query_parts = []
    key_accum = jnp.zeros((group_size, local_heads, HD), jnp.float32)
    value_accum = jnp.zeros((group_size, local_heads, HD), jnp.float32)
    for block_number in range(block_count):
        first_row = block_number * block_rows
        query_block, bent_scores, allowed = block_scores(first_row, query_all, key_copies)
        prob_full = jnp.where(
            allowed[None], jnp.exp(SOFT_CAP * bent_scores - log_totals[block_number]), 0.0
        )
        grad_block = grad_attended[first_row : first_row + block_rows]
        grad_probs = jnp.einsum(
            "qhd,khd->hqk", grad_block, value_copies, preferred_element_type=jnp.float32
        )
        inner_sum = jnp.sum(prob_full * grad_probs, axis=-1, keepdims=True)
        grad_raw = (
            prob_full * (grad_probs - inner_sum) * (1.0 - bent_scores * bent_scores) * qk_scale
        ).astype(jnp.bfloat16)
        query_parts.append(
            jnp.einsum("hqk,khd->qhd", grad_raw, key_copies, preferred_element_type=jnp.float32)
        )
        key_accum = key_accum + jnp.einsum(
            "hqk,qhd->khd", grad_raw, query_block, preferred_element_type=jnp.float32
        )
        value_accum = value_accum + jnp.einsum(
            "hqk,qhd->khd",
            prob_full.astype(jnp.bfloat16),
            grad_block,
            preferred_element_type=jnp.float32,
        )
    query_grads = (
        jnp.concatenate(query_parts, axis=0)
        .astype(jnp.bfloat16)
        .reshape(group_size, local_heads * HD)
    )
    key_grads = key_accum.astype(jnp.bfloat16).reshape(group_size, local_heads * HD)
    value_grads = value_accum.astype(jnp.bfloat16).reshape(group_size, local_heads * HD)
    grad_w_query = jnp.dot(attn_gathered.T, query_grads, preferred_element_type=jnp.float32)
    key_columns = (
        jnp.dot(attn_gathered.T, key_grads, preferred_element_type=jnp.float32)
        .reshape(model_width, local_kv, copies, HD)
        .sum(axis=2)
        .reshape(model_width, local_kv * HD)
    )
    value_columns = (
        jnp.dot(attn_gathered.T, value_grads, preferred_element_type=jnp.float32)
        .reshape(model_width, local_kv, copies, HD)
        .sum(axis=2)
        .reshape(model_width, local_kv * HD)
    )
    key_weight_copies = jnp.repeat(
        key_weight.reshape(model_width, local_kv, HD), copies, axis=1
    ).reshape(model_width, local_heads * HD)
    value_weight_copies = jnp.repeat(
        value_weight.reshape(model_width, local_kv, HD), copies, axis=1
    ).reshape(model_width, local_heads * HD)
    grads_joined = jnp.concatenate([query_grads, key_grads, value_grads], axis=1)
    weights_joined = jnp.concatenate([query_weight, key_weight_copies, value_weight_copies], axis=1)
    grad_normed_attn = lax.psum_scatter(
        jnp.dot(grads_joined, weights_joined.T, preferred_element_type=jnp.float32),
        "tensor",
        scatter_dimension=0,
        tiled=True,
    )
    grad_in_norm, gain_first = norm_back(stream, scale_in, norm_scale[0], grad_normed_attn)
    grad_tokens = grad_middle + grad_in_norm
    gain_stack = jnp.stack([gain_first, gain_second, gain_third, gain_last], axis=0)
    reduced = (
        lax.psum_scatter(grad_w_query, "dp", scatter_dimension=0, tiled=True),
        lax.psum_scatter(key_columns, "dp", scatter_dimension=0, tiled=True),
        lax.psum_scatter(value_columns, "dp", scatter_dimension=0, tiled=True),
        lax.psum_scatter(grad_w_out, "dp", scatter_dimension=1, tiled=True),
        lax.psum_scatter(grad_w_gate, "dp", scatter_dimension=0, tiled=True),
        lax.psum_scatter(grad_w_up, "dp", scatter_dimension=0, tiled=True),
        lax.psum_scatter(grad_down, "dp", scatter_dimension=1, tiled=True),
        lax.psum_scatter(gain_stack, "dp", scatter_dimension=1, tiled=True),
    )
    full_width = w_key.shape[1]
    shard_rows = reduced[1].shape[0]
    key_full = lax.dynamic_update_slice_in_dim(
        jnp.zeros((shard_rows, full_width), jnp.float32), reduced[1], kv_first * HD, 1
    )
    value_full = lax.dynamic_update_slice_in_dim(
        jnp.zeros((shard_rows, full_width), jnp.float32), reduced[2], kv_first * HD, 1
    )
    shared = lax.psum((key_full, value_full, reduced[7]), "tensor")
    return (
        result,
        grad_tokens,
        reduced[0],
        shared[0],
        shared[1],
        reduced[3],
        reduced[4],
        reduced[5],
        reduced[6],
        shared[2],
    )


def solution(mesh):
    in_specs = (
        P(("dp", "tensor"), None),
        P(("dp", "tensor"), None),
        P("dp", None),
        P("dp", "tensor"),
        P("dp", None),
        P("dp", None),
        P("tensor", "dp"),
        P("dp", "tensor"),
        P("dp", "tensor"),
        P("tensor", "dp"),
        P(None, "dp"),
    )
    out_specs = (
        P(("dp", "tensor"), None),
        P(("dp", "tensor"), None),
        P("dp", "tensor"),
        P("dp", None),
        P("dp", None),
        P("tensor", "dp"),
        P("dp", "tensor"),
        P("dp", "tensor"),
        P("tensor", "dp"),
        P(None, "dp"),
    )
    return jax.shard_map(shards, mesh=mesh, in_specs=in_specs, out_specs=out_specs, check_vma=False)
```

profile of v0, /device:TPU:0, one launch (start us, length us, event | category | flops | bytes accessed | tf_op | source)
XLA Modules:
  0.0 1836.3 jit_solution(9742927209121427723)
XLA Ops:
  9.0 15.8 all-gather
  35.8 39.4 %all-gather.13.cloned.1.call-done = bf16[512,2304]{1,0:T(8,128)(2,1)} async-done(((bf16[128,2304]{1,0:T(8,128)(2,1)}), bf16[512,2304]{1,0:T(8,128)(2,1)}) %all-gather.13.cloned.1.call-update) | async-done | bytes 2359312 | tf_op jit(solution)/shard_map/all_gather | solution.py:90
  78.3 22.0 %all-gather.15.cloned.1.call-done = bf16[2304,256]{1,0:T(8,128)(2,1)} async-done(((bf16[288,256]{1,0:T(8,128)(2,1)}), bf16[2304,256]{1,0:T(8,128)(2,1)}) %all-gather.15.cloned.1.call-update) | async-done | bytes 1179664 | tf_op jit(solution)/shard_map/all_gather | solution.py:48
  102.3 30.6 %all-gather.17.cloned.1.call-done = bf16[2304,512]{1,0:T(8,128)(2,1)} async-done(((bf16[288,512]{1,0:T(8,128)(2,1)}), bf16[2304,512]{1,0:T(8,128)(2,1)}) %all-gather.17.cloned.1.call-update) | async-done | bytes 2359312 | tf_op jit(solution)/shard_map/all_gather | solution.py:46
  139.1 25.9 %all-gather.21.cloned.1.call-done = bf16[512,2304]{0,1:T(8,128)(2,1)} async-done(((bf16[512,288]{0,1:T(8,128)(2,1)}), bf16[512,2304]{0,1:T(8,128)(2,1)}) %all-gather.21.cloned.1.call-update) | async-done | bytes 2359312 | tf_op jit(solution)/shard_map/all_gather | solution.py:49
  170.4 56.3 %reduce-scatter.15.cloned.1.call-done = f32[128,2304]{1,0:T(8,128)} async-done(((f32[512,2304]{1,0:T(8,128)}), f32[128,2304]{1,0:T(8,128)}) %reduce-scatter.15.cloned.1.call-update) | async-done | bytes 1179664 | tf_op jit(solution)/shard_map/reduce_scatter | solution.py:126
  233.5 34.8 %all-gather.23.cloned.1.call-done = bf16[512,2304]{1,0:T(8,128)(2,1)} async-done(((bf16[128,2304]{1,0:T(8,128)(2,1)}), bf16[512,2304]{1,0:T(8,128)(2,1)}) %all-gather.23.cloned.1.call-update) | async-done | bytes 2359312 | tf_op jit(solution)/shard_map/all_gather | solution.py:136
  268.3 102.1 %all-gather.25.cloned.1.call-done = bf16[2304,2304]{1,0:T(8,128)(2,1)} async-done(((bf16[288,2304]{1,0:T(8,128)(2,1)}), bf16[2304,2304]{1,0:T(8,128)(2,1)}) %all-gather.25.cloned.1.call-update) | async-done | bytes 10616848 | tf_op jit(solution)/shard_map/all_gather | solution.py:50
  370.5 11.6 fusion.112
  382.1 88.8 %all-gather.27.cloned.1.call-done = bf16[2304,2304]{1,0:T(8,128)(2,1)} async-done(((bf16[288,2304]{1,0:T(8,128)(2,1)}), bf16[2304,2304]{1,0:T(8,128)(2,1)}) %all-gather.27.cloned.1.call-update) | async-done | bytes 10616848 | tf_op jit(solution)/shard_map/all_gather | solution.py:51
  470.9 12.8 multiply_convert_fusion.1
  483.8 87.5 %all-gather.29.cloned.1.call-done = bf16[2304,2304]{0,1:T(8,128)(2,1)} async-done(((bf16[2304,288]{0,1:T(8,128)(2,1)}), bf16[2304,2304]{0,1:T(8,128)(2,1)}) %all-gather.29.cloned.1.call-update) | async-done | bytes 10616848 | tf_op jit(solution)/shard_map/all_gather | solution.py:52
  571.2 11.7 fusion.113
  583.0 55.4 %reduce-scatter.17.cloned.1.call-done = f32[128,2304]{1,0:T(8,128)} async-done(((f32[512,2304]{1,0:T(8,128)}), f32[128,2304]{1,0:T(8,128)}) %reduce-scatter.17.cloned.1.call-update) | async-done | bytes 1179664 | tf_op jit(solution)/shard_map/reduce_scatter | solution.py:140
  643.5 37.3 %all-gather.31.cloned.1.call-done = bf16[512,2304]{1,0:T(8,128)(2,1)} async-done(((bf16[128,2304]{1,0:T(8,128)(2,1)}), bf16[512,2304]{1,0:T(8,128)(2,1)}) %all-gather.31.cloned.1.call-update) | async-done | bytes 2359312 | tf_op jit(solution)/shard_map/all_gather | solution.py:150
  680.8 14.2 multiply_convert_fusion
  695.0 9.8 fusion.114
  704.9 11.3 convolution_add_fusion
  716.3 57.1 %reduce-scatter.19.cloned.1.call-done = f32[128,2304]{1,0:T(8,128)} async-done(((f32[512,2304]{1,0:T(8,128)}), f32[128,2304]{1,0:T(8,128)}) %reduce-scatter.19.cloned.1.call-update) | async-done | bytes 1179664 | tf_op jit(solution)/shard_map/reduce_scatter | solution.py:180
  778.3 37.2 %all-gather.33.cloned.1.call-done = bf16[512,2304]{1,0:T(8,128)(2,1)} async-done(((bf16[128,2304]{1,0:T(8,128)(2,1)}), bf16[512,2304]{1,0:T(8,128)(2,1)}) %all-gather.33.cloned.1.call-update) | async-done | bytes 2359312 | tf_op jit(solution)/shard_map/all_gather | solution.py:190
  869.9 57.6 %reduce-scatter.21.cloned.1.call-done = f32[128,2304]{1,0:T(8,128)} async-done(((f32[512,2304]{1,0:T(8,128)}), f32[128,2304]{1,0:T(8,128)}) %reduce-scatter.21.cloned.1.call-update) | async-done | bytes 1179664 | tf_op jit(solution)/shard_map/reduce_scatter | solution.py:254
  930.7 36.5 %reduce-scatter.27.cloned.1.call-done = f32[288,256]{1,0:T(8,128)} async-done(((f32[2304,256]{1,0:T(8,128)}), f32[288,256]{1,0:T(8,128)}) %reduce-scatter.27.cloned.1.call-update) | async-done | bytes 294928 | tf_op jit(solution)/shard_map/reduce_scatter | solution.py:266
  981.8 11.7 fusion.117
  993.7 11.8 fusion.118
  1007.1 12.1 fusion.119
  1023.2 10.4 psum.23
  1033.7 43.4 %all-reduce.3.cloned.1.call-done = (f32[288,1024]{1,0:T(8,128)}, f32[288,1024]{1,0:T(8,128)}) async-done(((f32[288,1024]{1,0:T(8,128)}, f32[288,1024]{1,0:T(8,128)}), (f32[288,1024]{1,0:T(8,128)}, f32[288,1024]{1,0:T(8,128)})) %all-reduce.3.cloned.1.call-update) | async-done | bytes 2359312 | tf_op jit(solution)/shard_map/psum | solution.py:281
  1077.1 57.6 %reduce-scatter.23.cloned.1.call-done = f32[288,512]{1,0:T(8,128)} async-done(((f32[2304,512]{1,0:T(8,128)}), f32[288,512]{1,0:T(8,128)}) %reduce-scatter.23.cloned.1.call-update) | async-done | bytes 589840 | tf_op jit(solution)/shard_map/reduce_scatter | solution.py:264
  1134.7 56.3 %reduce-scatter.29.cloned.1.call-done = f32[512,288]{0,1:T(8,128)} async-done(((f32[512,2304]{0,1:T(8,128)}), f32[512,288]{0,1:T(8,128)}) %reduce-scatter.29.cloned.1.call-update) | async-done | bytes 589840 | tf_op jit(solution)/shard_map/reduce_scatter | solution.py:267
  1191.0 211.5 %reduce-scatter.31.cloned.1.call-done = f32[288,2304]{1,0:T(8,128)} async-done(((f32[2304,2304]{1,0:T(8,128)}), f32[288,2304]{1,0:T(8,128)}) %reduce-scatter.31.cloned.1.call-update) | async-done | bytes 2654224 | tf_op jit(solution)/shard_map/reduce_scatter | solution.py:268
  1402.5 211.5 %reduce-scatter.33.cloned.1.call-done = f32[288,2304]{1,0:T(8,128)} async-done(((f32[2304,2304]{1,0:T(8,128)}), f32[288,2304]{1,0:T(8,128)}) %reduce-scatter.33.cloned.1.call-update) | async-done | bytes 2654224 | tf_op jit(solution)/shard_map/reduce_scatter | solution.py:269
  1614.0 211.4 %reduce-scatter.35.cloned.1.call-done = f32[2304,288]{0,1:T(8,128)} async-done(((f32[2304,2304]{0,1:T(8,128)}), f32[2304,288]{0,1:T(8,128)}) %reduce-scatter.35.cloned.1.call-update) | async-done | bytes 2654224 | tf_op jit(solution)/shard_map/reduce_scatter | solution.py:270
  (191 shorter events, 127.2 us)
Async XLA Ops:
  7.2 28.6 %all-gather.19.cloned.1.call-start = ((), (), s32[]{:S(2)}) async-start(), calls=%async_computation.15 | async-start | bytes 1327104 | tf_op jit(solution)/shard_map/all_gather | solution.py:47
  9.0 66.2 %all-gather.13.cloned.1.call-start = ((), (), s32[]{:S(2)}) async-start(), calls=%async_computation.12 | async-start | bytes 2949120 | tf_op jit(solution)/shard_map/all_gather | solution.py:90
  28.4 71.8 %all-gather.15.cloned.1.call-start = ((), (), s32[]{:S(2)}) async-start(), calls=%async_computation.13 | async-start | bytes 1327104 | tf_op jit(solution)/shard_map/all_gather | solution.py:48
  30.1 102.7 %all-gather.17.cloned.1.call-start = ((), (), s32[]{:S(2)}) async-start(), calls=%async_computation.14 | async-start | bytes 2654208 | tf_op jit(solution)/shard_map/all_gather | solution.py:46
  30.7 134.4 %all-gather.21.cloned.1.call-start = ((), (), s32[]{:S(2)}) async-start(), calls=%async_computation.16 | async-start | bytes 2654208 | tf_op jit(solution)/shard_map/all_gather | solution.py:49
  31.3 195.5 %reduce-scatter.15.cloned.1.call-start = ((), (), s32[]{:S(2)}) async-start(), calls=%async_computation.17 | async-start | bytes 5898240 | tf_op jit(solution)/shard_map/reduce_scatter | solution.py:126
  33.0 788.0 %copy-start.21 = (pred[512,512]{0,1:T(8,128)(4,1)}, pred[512,512]{0,1:T(8,128)(4,1)S(1)}, u32[]{:S(2)}) copy-start(pred[512,512]{0,1:T(8,128)(4,1)S(1)} %fusion.83) | copy-start | bytes 786436
  170.3 57.9 %copy-start.3 = (bf16[128,2304]{1,0:T(8,128)(2,1)S(1)}, bf16[128,2304]{1,0:T(8,128)(2,1)}, u32[]{:S(2)}) copy-start(bf16[128,2304]{1,0:T(8,128)(2,1)} %param.11) | copy-start | bytes 1769476
  170.3 98.0 %all-gather.23.cloned.1.call-start = ((), (), s32[]{:S(2)}) async-start(), calls=%async_computation.18 | async-start | bytes 2949120 | tf_op jit(solution)/shard_map/all_gather | solution.py:136
  230.9 139.6 %all-gather.25.cloned.1.call-start = ((), (), s32[]{:S(2)}) async-start(), calls=%async_computation.19 | async-start | bytes 11943936 | tf_op jit(solution)/shard_map/all_gather | solution.py:50
  231.6 239.3 %all-gather.27.cloned.1.call-start = ((), (), s32[]{:S(2)}) async-start(), calls=%async_computation.20 | async-start | bytes 11943936 | tf_op jit(solution)/shard_map/all_gather | solution.py:51
  232.3 338.9 %all-gather.29.cloned.1.call-start = ((), (), s32[]{:S(2)}) async-start(), calls=%async_computation.21 | async-start | bytes 11943936 | tf_op jit(solution)/shard_map/all_gather | solution.py:52
  232.9 405.5 %reduce-scatter.17.cloned.1.call-start = ((), (), s32[]{:S(2)}) async-start(), calls=%async_computation.22 | async-start | bytes 5898240 | tf_op jit(solution)/shard_map/reduce_scatter | solution.py:140
  582.9 97.9 %all-gather.31.cloned.1.call-start = ((), (), s32[]{:S(2)}) async-start(), calls=%async_computation.23 | async-start | bytes 2949120 | tf_op jit(solution)/shard_map/all_gather | solution.py:150
  643.3 130.0 %reduce-scatter.19.cloned.1.call-start = ((), (), s32[]{:S(2)}) async-start(), calls=%async_computation.24 | async-start | bytes 5898240 | tf_op jit(solution)/shard_map/reduce_scatter | solution.py:180
  716.2 58.9 %copy-start.2 = (f32[128,2304]{1,0:T(8,128)S(1)}, f32[128,2304]{1,0:T(8,128)}, u32[]{:S(2)}) copy-start(f32[128,2304]{1,0:T(8,128)} %reduce-scatter.15.cloned.1.call-done) | copy-start | bytes 3538948
  716.2 99.2 %all-gather.33.cloned.1.call-start = ((), (), s32[]{:S(2)}) async-start(), calls=%async_computation.25 | async-start | bytes 2949120 | tf_op jit(solution)/shard_map/all_gather | solution.py:190
  778.0 90.8 %reduce-scatter.25.cloned.1.call-start = ((), (), s32[]{:S(2)}) async-start(), calls=%async_computation.28 | async-start | bytes 2654208 | tf_op jit(solution)/shard_map/reduce_scatter | solution.py:265
  831.5 95.9 %reduce-scatter.21.cloned.1.call-start = ((), (), s32[]{:S(2)}) async-start(), calls=%async_computation.26 | async-start | bytes 5898240 | tf_op jit(solution)/shard_map/reduce_scatter | solution.py:254
  856.2 111.1 %reduce-scatter.27.cloned.1.call-start = ((), (), s32[]{:S(2)}) async-start(), calls=%async_computation.29 | async-start | bytes 2654208 | tf_op jit(solution)/shard_map/reduce_scatter | solution.py:266
  860.0 67.5 %copy-start.4 = (bf16[128,2304]{1,0:T(8,128)(2,1)S(1)}, bf16[128,2304]{1,0:T(8,128)(2,1)}, u32[]{:S(2)}) copy-start(bf16[128,2304]{1,0:T(8,128)(2,1)} %param.11) | copy-start | bytes 1769476
  860.0 67.5 %copy-start.24 = (f32[2304]{0:T(1024)S(1)}, f32[2304]{0:T(1024)}, u32[]{:S(2)}) copy-start(f32[2304]{0:T(1024)} %copy-done.23) | copy-start | bytes 27652
  860.0 67.5 %copy-start.26 = (f32[128]{0:T(128)S(1)}, f32[128]{0:T(128)}, u32[]{:S(2)}) copy-start(f32[128]{0:T(128)} %copy-done.25) | copy-start | bytes 1540
  860.1 162.2 %reduce-scatter.37.cloned.1.call-start = ((), (), s32[]{:S(2)}) async-start(), calls=%async_computation.34 | async-start | bytes 1327104
  869.9 60.8 %copy-start.10 = (f32[288,1024]{1,0:T(8,128)}, f32[288,1024]{1,0:T(8,128)S(1)}, u32[]{:S(2)}) copy-start(f32[288,1024]{1,0:T(8,128)S(1)} %constant_dynamic-update-slice_fusion.1) | copy-start | bytes 3538948
  930.7 146.4 %all-reduce.3.cloned.1.call-start = ((), (), s32[]{:S(2)}) async-start(), calls=%async_computation.35 | async-start | bytes 4718592 | tf_op jit(solution)/shard_map/psum | solution.py:281
  969.5 165.2 %reduce-scatter.23.cloned.1.call-start = ((), (), s32[]{:S(2)}) async-start(), calls=%async_computation.27 | async-start | bytes 5308416 | tf_op jit(solution)/shard_map/reduce_scatter | solution.py:264
  974.8 216.2 %reduce-scatter.29.cloned.1.call-start = ((), (), s32[]{:S(2)}) async-start(), calls=%async_computation.30 | async-start | bytes 5308416 | tf_op jit(solution)/shard_map/reduce_scatter | solution.py:267
  980.2 422.3 %reduce-scatter.31.cloned.1.call-start = ((), (), s32[]{:S(2)}) async-start(), calls=%async_computation.31 | async-start | bytes 23887872 | tf_op jit(solution)/shard_map/reduce_scatter | solution.py:268
  993.6 620.4 %reduce-scatter.33.cloned.1.call-start = ((), (), s32[]{:S(2)}) async-start(), calls=%async_computation.32 | async-start | bytes 23887872 | tf_op jit(solution)/shard_map/reduce_scatter | solution.py:269
  1005.4 820.0 %reduce-scatter.35.cloned.1.call-start = ((), (), s32[]{:S(2)}) async-start(), calls=%async_computation.33 | async-start | bytes 23887872 | tf_op jit(solution)/shard_map/reduce_scatter | solution.py:270
  1077.1 750.8 %copy-start.20 = (f32[288,1024]{1,0:T(8,128)S(1)}, f32[288,1024]{1,0:T(8,128)}, u32[]{:S(2)}) copy-start(f32[288,1024]{1,0:T(8,128)} %get-tuple-element.39) | copy-start | bytes 3538948
  (29 other events, 354.3 us)
Sparse Core Ops, SparseCore 0:
  10.2 25.4 all-gather.18
  38.2 36.9 all-gather.12
  77.4 22.7 all-gather.14
  101.7 31.0 all-gather.16
  134.3 30.6 all-gather.20
  170.5 56.2 reduce-scatter.14
  231.0 37.3 all-gather.22
  270.0 100.4 all-gather.24
  372.1 98.7 all-gather.26
  472.4 98.7 all-gather.28
  583.1 55.2 reduce-scatter.16
  643.4 37.3 all-gather.30
  716.4 56.9 reduce-scatter.18
  778.1 37.3 all-gather.32
  831.7 37.0 reduce-scatter.24
  871.6 55.8 reduce-scatter.20
  930.2 36.9 reduce-scatter.26
  969.4 31.8 reduce-scatter.36
  1005.0 72.0 all-reduce.2
  1079.8 54.8 reduce-scatter.22
  1137.6 53.3 reduce-scatter.28
  1193.9 208.5 reduce-scatter.30
  1405.4 208.5 reduce-scatter.32
  1616.8 208.5 reduce-scatter.34
where the time goes:
time: 1840 us
  waiting for transfers between devices  1570 us (85%)
  matrix products  166 us (9%)
  local copies, waits for them, and re-layouts  31.4 us (2%)
  blocking collectives  26.3 us (1%)
  other arithmetic  20.2 us (1%)
    reduce_scatter x1, waiting for transfers between devices, shards(): lax.psum_scatter(grad_w_up, 'dp', scatter_dimension=0, tiled=True)  212 us
    reduce_scatter x1, waiting for transfers between devices, shards(): lax.psum_scatter(grad_w_gate, 'dp', scatter_dimension=0, tiled=True)  212 us
    reduce_scatter x1, waiting for transfers between devices, shards(): lax.psum_scatter(grad_down, 'dp', scatter_dimension=1, tiled=True)  211 us
    all_gather x1, waiting for transfers between devices, shards(): lax.all_gather(w_gate, 'dp', axis=0, tiled=True)  102 us
    all_gather x1, waiting for transfers between devices, shards(): lax.all_gather(w_up, 'dp', axis=0, tiled=True)  88.8 us
    all_gather x1, waiting for transfers between devices, shards(): lax.all_gather(w_down, 'dp', axis=1, tiled=True)  87.5 us
    reduce_scatter x1, waiting for transfers between devices, shards(): lax.psum_scatter(grad_w_query, 'dp', scatter_dimension=0, tiled=True)  57.6 us
    reduce_scatter x1, waiting for transfers between devices, shards(): lax.psum_scatter(jnp.dot(grads_joined, weights_joined.T, preferred_elemen...  57.6 us
  transfers between devices with their start and end apart: 24, of which 23 were waited for; matrix products, arithmetic and copies ran while one was open for 7% of the time, Pallas kernels for 0%

commit v1 on v0

v1 whole, which is shorter than its diff:
```python
import jax
import jax.numpy as jnp
from jax import lax
from jax.sharding import PartitionSpec as P

HQ = 8
KVH = 4
HD = 256

EPSILON = 1e-06
SOFT_CAP = 50.0
BF = jnp.bfloat16
F32 = jnp.float32
BOTH = ("dp", "tensor")


def inv_root(source):
    return lax.rsqrt(jnp.mean(source * source, axis=-1, keepdims=True) + EPSILON)


def norm_back(source, inverse, gain_row, upstream):
    unit_rows = source * inverse
    scaled = upstream * gain_row
    grad_input = inverse * (
        scaled - unit_rows * jnp.mean(scaled * unit_rows, axis=-1, keepdims=True)
    )
    return (grad_input, jnp.sum(upstream * unit_rows, axis=0))


def gated_unit(gate_in, up_in):
    return jax.nn.gelu(gate_in, approximate=True) * up_in


def dot_nn(left, right):
    return jnp.dot(left, right, preferred_element_type=F32)


def dot_nt(left, right):
    return lax.dot_general(left, right, (((1,), (1,)), ((), ())), preferred_element_type=F32)


def dot_tn(left, right):
    return lax.dot_general(left, right, (((0,), (0,)), ((), ())), preferred_element_type=F32)


class Grid:
    def __init__(self, dp, tp):
        self.dp, self.tp = dp, tp
        self.nz, self.nc = dp // 2, 2
        self.ny, self.nx = 2, tp // 2

    def coords(self, flat):
        d, t = divmod(flat, self.tp)
        z, c = divmod(d, self.nc)
        y, x = divmod(t, self.nx)
        return z, c, y, x

    def flat(self, z, c, y, x):
        return (z * self.nc + c) * self.tp + y * self.nx + x

    def move(self, value, where):
        pairs = []
        for i in range(self.dp * self.tp):
            pairs.append((i, self.flat(*where(*self.coords(i)))))
        return lax.ppermute(value, BOTH, pairs)

    def rot_z(self, value, k=1):
        return self.move(value, lambda z, c, y, x: ((z + k) % self.nz, c, y, x))

    def swap_c(self, value):
        return self.move(value, lambda z, c, y, x: (z, 1 - c, y, x))

    def swap_y(self, value):
        return self.move(value, lambda z, c, y, x: (z, c, 1 - y, x))

    def xor_x(self, value, k):
        return self.move(value, lambda z, c, y, x: (z, c, y, x ^ k))

    def xor_t(self, value, k):
        def where(z, c, y, x):
            t = (y * self.nx + x) ^ k
            return z, c, t // self.nx, t % self.nx

        return self.move(value, where)

    def xor_dp(self, value, k):
        def where(z, c, y, x):
            d = (z * self.nc + c) ^ k
            return d // self.nc, d % self.nc, y, x

        return self.move(value, where)


def pick(stack, index, axis=0):
    return lax.dynamic_index_in_dim(stack, index, axis, keepdims=False)


def put(buffer, piece, *indices):
    start = tuple(indices) + (0,) * (buffer.ndim - len(indices))
    shaped = piece.reshape((1,) * len(indices) + piece.shape)
    return lax.dynamic_update_slice(buffer, shaped, start)


def program(
    grid,
    tokens,
    cotangent,
    doc_lengths,
    w_query,
    w_key,
    w_value,
    w_out,
    w_gate,
    w_up,
    w_down,
    norm_gains,
):
    nz, tp, nx = grid.nz, grid.tp, grid.nx
    dp_index = lax.axis_index("dp")
    t_index = lax.axis_index("tensor")
    z, c = dp_index // grid.nc, dp_index % grid.nc
    rows, width = tokens.shape
    dpart = w_query.shape[0]
    hidden_part = w_gate.shape[1]
    slot = hidden_part // nz
    group_size = rows * tp
    local_heads = w_query.shape[1] // HD
    local_kv = max(1, local_heads * KVH // HQ)
    copies = local_heads // local_kv
    kv_first = t_index * (local_heads * KVH) // HQ
    q_cols, kv_cols = local_heads * HD, local_kv * HD
    from_z = [(z - k) % nz for k in range(nz)]

    gains_other = grid.swap_c(norm_gains)
    gain_pair = jnp.where(
        c == 0, jnp.stack([norm_gains, gains_other]), jnp.stack([gains_other, norm_gains])
    )
    gain_buffer = jnp.zeros((nz,) + gain_pair.shape, BF)
    for k in range(nz):
        gain_buffer = put(gain_buffer, gain_pair if k == 0 else grid.rot_z(gain_pair, k), from_z[k])
    norm_scale = jnp.transpose(gain_buffer, (2, 0, 1, 3)).reshape(4, width).astype(F32)

    key_part = lax.dynamic_slice_in_dim(w_key, kv_first * HD, kv_cols, 1)
    value_part = lax.dynamic_slice_in_dim(w_value, kv_first * HD, kv_cols, 1)

    def gather_dp(local):
        pieces = [local]
        for k in range(1, nz):
            pieces.append(grid.rot_z(pieces[-1]))
        buffer = jnp.zeros((nz, 2) + local.shape, BF)
        for k in range(nz):
            buffer = put(buffer, pieces[k], from_z[k], c)
            buffer = put(buffer, grid.swap_c(pieces[k]), from_z[k], 1 - c)
        return buffer.reshape(width, local.shape[1]), pieces[-1]

    qkv_weight, last_piece = gather_dp(jnp.concatenate([w_query, key_part, value_part], axis=1))
    out_local, last_piece = lax.optimization_barrier((w_out.T, last_piece))
    out_weight_t, last_piece = gather_dp(out_local)

    def by_slot(matrix):
        return jnp.transpose(matrix.reshape(dpart, nz, slot), (1, 0, 2))

    down_slots = jnp.transpose(w_down.reshape(nz, slot, dpart), (0, 2, 1))
    slots, last_piece = lax.optimization_barrier(
        ((by_slot(w_gate), by_slot(w_up), down_slots), last_piece)
    )

    def spread(stack):
        buffer = jnp.zeros((nz, 2, dpart, nx * slot), BF)
        for k in range(nz):
            mine = pick(stack, (z + k) % nz)
            piece = mine if k == 0 else grid.rot_z(mine, k)
            joined = jnp.concatenate(
                [piece] + [grid.xor_x(piece, j) for j in range(1, nx)], axis=1
            )
            buffer = put(buffer, joined, from_z[k], c)
            buffer = put(buffer, grid.swap_c(joined), from_z[k], 1 - c)
        return buffer.reshape(width, nx * slot)

    gate_weight, up_weight, down_weight_t = (spread(stack) for stack in slots)

    place_parts = [(t_index ^ k) * rows + jnp.arange(rows, dtype=jnp.int32) for k in range(tp)]
    places = jnp.concatenate(place_parts)
    doc_ends = jnp.cumsum(doc_lengths[0])
    inside = jnp.sum((doc_ends[None, :] <= places[:, None]).astype(jnp.int32), axis=1)
    segment = jnp.where(places >= doc_ends[-1], doc_lengths.shape[1] + places, inside)
    block_count = max(1, group_size // 512)
    block_rows = group_size // block_count
    qk_scale = HD ** (-0.5)

    def gather_t(unit):
        return jnp.concatenate([unit] + [grid.xor_t(unit, k) for k in range(1, tp)], axis=0)

    def scatter_t(partial):
        total = partial[:rows]
        for k in range(1, tp):
            total = total + grid.xor_t(partial[k * rows : (k + 1) * rows].astype(BF), k).astype(F32)
        return total

    def block_scores(first_row, query_all, key_copies):
        query_block = query_all[first_row : first_row + block_rows]
        raw_scores = jnp.einsum(
            "qhd,khd->hqk", query_block, key_copies, preferred_element_type=F32
        )
        bent_scores = jnp.tanh(raw_scores * (qk_scale / SOFT_CAP))
        row_segment = segment[first_row : first_row + block_rows]
        row_places = places[first_row : first_row + block_rows]
        allowed = (row_segment[:, None] == segment[None, :]) & (
            places[None, :] <= row_places[:, None]
        )
        return (query_block, bent_scores, allowed)

    stream = tokens.astype(F32)
    scale_in = inv_root(stream)
    normed_attn = (stream * scale_in * norm_scale[0]).astype(BF)
    attn_gathered = gather_t(normed_attn)
    qkv = dot_nn(attn_gathered, qkv_weight).astype(BF)
    query_all = qkv[:, :q_cols].reshape(group_size, local_heads, HD)
    key_heads = qkv[:, q_cols : q_cols + kv_cols].reshape(group_size, local_kv, HD)
    value_heads = qkv[:, q_cols + kv_cols :].reshape(group_size, local_kv, HD)
    key_copies = jnp.repeat(key_heads, copies, axis=1)
    value_copies = jnp.repeat(value_heads, copies, axis=1)
    head_outs = []
    log_totals = []
    for block_number in range(block_count):
        first_row = block_number * block_rows
        query_block, bent_scores, allowed = block_scores(first_row, query_all, key_copies)
        exp_scores = jnp.where(allowed[None], jnp.exp(SOFT_CAP * bent_scores), 0.0)
        row_total = jnp.sum(exp_scores, axis=-1, keepdims=True)
        prob_rows = (exp_scores / row_total).astype(BF)
        head_outs.append(
            jnp.einsum("hqk,khd->qhd", prob_rows, value_copies, preferred_element_type=F32)
        )
        log_totals.append(jnp.log(row_total))
    attended = jnp.concatenate(head_outs, axis=0).astype(BF).reshape(group_size, q_cols)
    attn_mixed = scatter_t(dot_nt(attended, out_weight_t))
    scale_mix = inv_root(attn_mixed)
    middle = stream + attn_mixed * scale_mix * norm_scale[1]
    scale_mid = inv_root(middle)
    normed_ffn = (middle * scale_mid * norm_scale[2]).astype(BF)

    def ring(unit, work):
        units, chunks, partials = unit, [], []
        for k in range(nz):
            chunk = jnp.concatenate([units, grid.swap_y(units)], axis=0)
            if k + 1 < nz:
                units = grid.rot_z(units)
            chunks.append(chunk)
            partial = work(k, chunk)
            partials.append(
                partial[:rows] + grid.swap_y(partial[rows:].astype(BF)).astype(F32)
            )
        total = partials[1 % nz]
        for k in range(2, nz + 1):
            total = grid.rot_z(total.astype(BF)).astype(F32) + partials[k % nz]
        return total, chunks

    gates, ups, hiddens = [], [], []

    def forward_work(k, chunk):
        gate_out = dot_nn(chunk, gate_weight)
        up_out = dot_nn(chunk, up_weight)
        hidden = gated_unit(gate_out, up_out).astype(BF)
        gates.append(gate_out)
        ups.append(up_out)
        hiddens.append(hidden)
        return dot_nt(hidden, down_weight_t)

    branch, ffn_chunks = ring(normed_ffn, forward_work)
    scale_ffn = inv_root(branch)
    result = middle + branch * scale_ffn * norm_scale[3]
    upstream = cotangent.astype(F32)
    grad_branch, gain_last = norm_back(branch, scale_ffn, norm_scale[3], upstream)

    grad_gates, grad_ups = [], []

    def backward_work(k, chunk):
        grad_hidden = dot_nn(chunk, down_weight_t)
        unused_value, pullback = jax.vjp(gated_unit, gates[k], ups[k])
        grad_gate_out, grad_up_out = pullback(grad_hidden)
        grad_gate_out = grad_gate_out.astype(BF)
        grad_up_out = grad_up_out.astype(BF)
        grad_gates.append(grad_gate_out)
        grad_ups.append(grad_up_out)
        return dot_nt(grad_gate_out, gate_weight) + dot_nt(grad_up_out, up_weight)

    grad_normed_ffn, branch_chunks = ring(grad_branch.astype(BF), backward_work)

    ffn_all = jnp.concatenate(ffn_chunks, axis=0)
    grad_down_t = dot_tn(
        jnp.concatenate(branch_chunks, axis=0), jnp.concatenate(hiddens, axis=0)
    ).astype(BF)
    grad_w_gate = dot_tn(ffn_all, jnp.concatenate(grad_gates, axis=0)).astype(BF)
    grad_w_up = dot_tn(ffn_all, jnp.concatenate(grad_ups, axis=0)).astype(BF)

    def core_sum(grads):
        stack = grads.reshape(nz, 2, dpart, grads.shape[1])
        other = grid.swap_c(pick(stack, 1 - c, 1))
        return pick(stack, c, 1).astype(F32) + other.astype(F32)

    def collect(grads):
        total = core_sum(grads)
        kept = total[:, :, :slot]
        for j in range(1, nx):
            sent = total[:, :, j * slot : (j + 1) * slot].astype(BF)
            kept = kept + grid.xor_x(sent, j).astype(F32)
        kept = kept.astype(BF)
        buffer = jnp.zeros((nz, dpart, slot), BF)
        for k in range(nz):
            piece = pick(kept, (z + k) % nz)
            buffer = put(buffer, piece if k == 0 else grid.rot_z(piece, k), from_z[k])
        return buffer

    def rows_of(buffer):
        return jnp.transpose(buffer, (1, 0, 2)).reshape(dpart, hidden_part).astype(F32)

    down_buffer = collect(grad_down_t)
    grad_down = jnp.transpose(down_buffer, (0, 2, 1)).reshape(hidden_part, dpart).astype(F32)
    grad_gate = rows_of(collect(grad_w_gate))
    grad_up = rows_of(collect(grad_w_up))

    grad_mid_norm, gain_third = norm_back(middle, scale_mid, norm_scale[2], grad_normed_ffn)
    grad_middle = upstream + grad_mid_norm
    grad_mixed, gain_second = norm_back(attn_mixed, scale_mix, norm_scale[1], grad_middle)
    mixed_grads = gather_t(grad_mixed.astype(BF))
    grad_out_t = dot_tn(mixed_grads, attended).astype(BF)
    grad_attended = (
        dot_nn(mixed_grads, out_weight_t).astype(BF).reshape(group_size, local_heads, HD)
    )
    query_parts = []
    key_accum = jnp.zeros((group_size, local_heads, HD), F32)
    value_accum = jnp.zeros((group_size, local_heads, HD), F32)
    for block_number in range(block_count):
        first_row = block_number * block_rows
        query_block, bent_scores, allowed = block_scores(first_row, query_all, key_copies)
        prob_full = jnp.where(
            allowed[None], jnp.exp(SOFT_CAP * bent_scores - log_totals[block_number]), 0.0
        )
        grad_block = grad_attended[first_row : first_row + block_rows]
        grad_probs = jnp.einsum(
            "qhd,khd->hqk", grad_block, value_copies, preferred_element_type=F32
        )
        inner_sum = jnp.sum(prob_full * grad_probs, axis=-1, keepdims=True)
        grad_raw = (
            prob_full * (grad_probs - inner_sum) * (1.0 - bent_scores * bent_scores) * qk_scale
        ).astype(BF)
        query_parts.append(
            jnp.einsum("hqk,khd->qhd", grad_raw, key_copies, preferred_element_type=F32)
        )
        key_accum = key_accum + jnp.einsum(
            "hqk,qhd->khd", grad_raw, query_block, preferred_element_type=F32
        )
        value_accum = value_accum + jnp.einsum(
            "hqk,qhd->khd", prob_full.astype(BF), grad_block, preferred_element_type=F32
        )
    query_grads = jnp.concatenate(query_parts, axis=0).astype(BF).reshape(group_size, q_cols)
    key_grads = key_accum.astype(BF).reshape(group_size, q_cols)
    value_grads = value_accum.astype(BF).reshape(group_size, q_cols)

    def fold(columns):
        return columns.reshape(width, local_kv, copies, HD).sum(axis=2).reshape(width, kv_cols)

    key_columns = fold(dot_tn(attn_gathered, key_grads)).astype(BF)
    value_columns = fold(dot_tn(attn_gathered, value_grads)).astype(BF)
    grad_w_query = dot_tn(attn_gathered, query_grads).astype(BF)

    def widen(weight):
        return jnp.repeat(weight.reshape(width, local_kv, HD), copies, axis=1).reshape(
            width, q_cols
        )

    grads_joined = jnp.concatenate([query_grads, key_grads, value_grads], axis=1)
    weights_joined = jnp.concatenate(
        [
            qkv_weight[:, :q_cols],
            widen(qkv_weight[:, q_cols : q_cols + kv_cols]),
            widen(qkv_weight[:, q_cols + kv_cols :]),
        ],
        axis=1,
    )
    grad_normed_attn = scatter_t(dot_nt(grads_joined, weights_joined))
    grad_in_norm, gain_first = norm_back(stream, scale_in, norm_scale[0], grad_normed_attn)
    grad_tokens = grad_middle + grad_in_norm

    def ring_sum(grads):
        stack = core_sum(grads)
        total = pick(stack, from_z[1 % nz])
        for k in range(2, nz + 1):
            total = grid.rot_z(total.astype(BF)).astype(F32) + pick(stack, from_z[k % nz])
        return total

    grad_out = ring_sum(grad_out_t).T
    kv_sum = ring_sum(jnp.concatenate([key_columns, value_columns], axis=1)).astype(BF)
    grad_query = ring_sum(grad_w_query)

    kv_buffer = jnp.zeros((tp,) + kv_sum.shape, BF)
    for k in range(tp):
        kv_buffer = put(kv_buffer, kv_sum if k == 0 else grid.xor_t(kv_sum, k), t_index ^ k)
    sharers = tp * local_kv // KVH
    kv_full = kv_buffer.astype(F32).reshape(tp // sharers, sharers, dpart, 2, kv_cols).sum(axis=1)
    kv_full = jnp.transpose(kv_full, (2, 1, 0, 3)).reshape(2, dpart, KVH * HD)

    gain_stack = jnp.stack([gain_first, gain_second, gain_third, gain_last], axis=0)
    gain_parts = jnp.transpose(gain_stack.reshape(4, grid.dp, dpart), (1, 0, 2))
    gain_sum = pick(gain_parts, dp_index)
    for k in range(1, grid.dp):
        gain_sum = gain_sum + grid.xor_dp(pick(gain_parts, dp_index ^ k), k)
    gain_table = jnp.zeros((tp,) + gain_sum.shape, F32)
    for k in range(tp):
        gain_table = put(gain_table, gain_sum if k == 0 else grid.xor_t(gain_sum, k), t_index ^ k)
    grad_gains = gain_table.sum(axis=0)

    return (
        result,
        grad_tokens,
        grad_query,
        kv_full[0],
        kv_full[1],
        grad_out,
        grad_gate,
        grad_up,
        grad_down,
        grad_gains,
    )


def solution(mesh):
    grid = Grid(mesh.shape["dp"], mesh.shape["tensor"])

    def shards(*args):
        return program(grid, *args)

    in_specs = (
        P(("dp", "tensor"), None),
        P(("dp", "tensor"), None),
        P("dp", None),
        P("dp", "tensor"),
        P("dp", None),
        P("dp", None),
        P("tensor", "dp"),
        P("dp", "tensor"),
        P("dp", "tensor"),
        P("tensor", "dp"),
        P(None, "dp"),
    )
    out_specs = (
        P(("dp", "tensor"), None),
        P(("dp", "tensor"), None),
        P("dp", "tensor"),
        P("dp", None),
        P("dp", None),
        P("tensor", "dp"),
        P("dp", "tensor"),
        P("dp", "tensor"),
        P("tensor", "dp"),
        P(None, "dp"),
    )
    return jax.shard_map(shards, mesh=mesh, in_specs=in_specs, out_specs=out_specs, check_vma=False)
```

time: 1840 us -> 880 us (0.48)
  waiting for transfers between devices: 1570 us -> 377 us
  local copies, waits for them, and re-layouts: 31.4 us -> 182 us
  starting transfers between devices: 2.43 us -> 130 us
  matrix products: 166 us -> 129 us
  blocking collectives: 26.3 us -> 0 us
  other arithmetic: 20.2 us -> 42.5 us
    reduce_scatter x11 -> x0, waiting for transfers between devices: 1020 us -> none  [the longest x1 212 us: shards(): lax.psum_scatter(grad_w_up, 'dp', scatter_dimension=0, tiled=True)]
    all_gather x11 -> x0, waiting for transfers between devices: 508 us -> none  [the longest x1 102 us: shards(): lax.all_gather(w_gate, 'dp', axis=0, tiled=True)]
    ppermute x0 -> x131, waiting for transfers between devices: none -> 377 us  [move(): return lax.ppermute(value, BOTH, pairs)]
    ppermute x0 -> x131, starting transfers between devices: none -> 130 us  [move(): return lax.ppermute(value, BOTH, pairs)]
    dynamic_update_slice x2 -> x46, local copies, waits for them, and re-layouts: 1.99 us -> 73.1 us  [put(): return lax.dynamic_update_slice(buffer, shaped, start)]
    psum x1 -> x0, waiting for transfers between devices: 43.4 us -> none  [shards(): shared = lax.psum((key_full, value_full, reduced[7]), 'tensor')]
    dot_general x24 -> x40, matrix products: 165 us -> 127 us  [the longest x14 41.4 us: dot_nn(): return jnp.dot(left, right, preferred_element_type=F32)]
  transfers between devices with their start and end apart: 24 -> 131, of which waited for: 23 -> 57; matrix products, arithmetic and copies ran while one was open for 7% -> 33% of each run, Pallas kernels for 0% -> 0%
where the time goes in v1:
time: 880 us; the launch traced here: 864 us
  waiting for transfers between devices  377 us (43%)
  local copies, waits for them, and re-layouts  182 us (21%)
  starting transfers between devices  130 us (15%)
  matrix products  129 us (15%)
  other arithmetic  42.5 us (5%)
    ppermute x131, waiting for transfers between devices, move(): return lax.ppermute(value, BOTH, pairs)  377 us
    ppermute x131, starting transfers between devices, move(): return lax.ppermute(value, BOTH, pairs)  130 us
    dynamic_update_slice x46, local copies, waits for them, and re-layouts, put(): return lax.dynamic_update_slice(buffer, shaped, start)  73.1 us
    dot_general x14, matrix products, dot_nn(): return jnp.dot(left, right, preferred_element_type=F32)  41.4 us
    dot_general x7, matrix products, dot_tn(): lax.dot_general(left, right, (((0,), (0,)), ((), ())), preferred_element_...  37.9 us
    dot_general x14, matrix products, dot_nt(): lax.dot_general(left, right, (((1,), (1,)), ((), ())), preferred_element_...  32.8 us
    unnamed x210, local copies, waits for them, and re-layouts  27.9 us
  transfers between devices with their start and end apart: 131, of which 57 were waited for; matrix products, arithmetic and copies ran while one was open for 33% of the time, Pallas kernels for 0%

profile of v1, /device:TPU:0, one launch (start us, length us, event | category | flops | bytes accessed | tf_op | source)
XLA Modules:
  0.0 864.2 jit_solution(2286368578863791011)
XLA Ops:
  40.8 8.9 %collective-permute-done.10 = bf16[288,1024]{1,0:T(8,128)(2,1)} collective-permute-done((bf16[288,1024]{1,0:T(8,128)(2,1)}, bf16[288,1024]{1,0:T(8,128)(2,1)}, u32[]{:S(2)}, u32[]{:S(2)}) %collective-permute-start.10) | collective-permute-done | bytes 589856 | tf_op jit(solution)/shard_map/ppermute | solution.py:65
  55.6 11.3 %collective-permute-done.12 = bf16[288,1024]{1,0:T(8,128)(2,1)S(1)} collective-permute-done((bf16[288,1024]{1,0:T(8,128)(2,1)}, bf16[288,1024]{1,0:T(8,128)(2,1)S(1)}, u32[]{:S(2)}, u32[]{:S(2)}) %collective-permute-start.12) | collective-permute-done | bytes 589856 | tf_op jit(solution)/shard_map/ppermute | solution.py:65
  71.5 6.6 collective-permute-done.15
  82.1 7.3 collective-permute-done.17
  143.0 12.0 %collective-permute-done.21 = bf16[128,2304]{1,0:T(8,128)(2,1)S(1)} collective-permute-done((bf16[128,2304]{1,0:T(8,128)(2,1)S(1)}, bf16[128,2304]{1,0:T(8,128)(2,1)S(1)}, u32[]{:S(2)}, u32[]{:S(2)}) %collective-permute-start.21) | collective-permute-done | bytes 589856 | tf_op jit(solution)/shard_map/ppermute | solution.py:65
  155.0 12.2 %collective-permute-done.23 = bf16[128,2304]{1,0:T(8,128)(2,1)S(1)} collective-permute-done((bf16[128,2304]{1,0:T(8,128)(2,1)S(1)}, bf16[128,2304]{1,0:T(8,128)(2,1)S(1)}, u32[]{:S(2)}, u32[]{:S(2)}) %collective-permute-start.23) | collective-permute-done | bytes 589856 | tf_op jit(solution)/shard_map/ppermute | solution.py:65
  174.8 7.8 collective-permute-done.50
  185.5 8.5 collective-permute-done.40
  194.1 6.7 collective-permute-start.42
  203.9 17.0 %collective-permute-done.24 = bf16[128,2304]{1,0:T(8,128)(2,1)S(1)} collective-permute-done((bf16[128,2304]{1,0:T(8,128)(2,1)S(1)}, bf16[128,2304]{1,0:T(8,128)(2,1)S(1)}, u32[]{:S(2)}, u32[]{:S(2)}) %collective-permute-start.24) | collective-permute-done | bytes 589856 | tf_op jit(solution)/shard_map/ppermute | solution.py:65
  223.0 7.1 collective-permute-start.45
  235.1 21.4 %collective-permute-done.53 = bf16[288,576]{1,0:T(8,128)(2,1)S(1)} collective-permute-done((bf16[288,576]{1,0:T(8,128)(2,1)S(1)}, bf16[288,576]{1,0:T(8,128)(2,1)S(1)}, u32[]{:S(2)}, u32[]{:S(2)}) %collective-permute-start.53) | collective-permute-done | bytes 331808 | tf_op jit(solution)/shard_map/ppermute | solution.py:65
  268.0 6.9 collective-permute-start.61
  275.3 14.1 %collective-permute-done.61 = bf16[128,2304]{1,0:T(8,128)(2,1)S(1)} collective-permute-done((bf16[128,2304]{1,0:T(8,128)(2,1)S(1)}, bf16[128,2304]{1,0:T(8,128)(2,1)S(1)}, u32[]{:S(2)}, u32[]{:S(2)}) %collective-permute-start.61) | collective-permute-done | bytes 589856 | tf_op jit(solution)/shard_map/ppermute | solution.py:65
  293.9 15.3 %collective-permute-done.65 = bf16[128,2304]{1,0:T(8,128)(2,1)S(1)} collective-permute-done((bf16[128,2304]{1,0:T(8,128)(2,1)S(1)}, bf16[128,2304]{1,0:T(8,128)(2,1)S(1)}, u32[]{:S(2)}, u32[]{:S(2)}) %collective-permute-start.65) | collective-permute-done | bytes 589856 | tf_op jit(solution)/shard_map/ppermute | solution.py:65
  410.8 15.6 %collective-permute-done.72 = bf16[128,2304]{1,0:T(8,128)(2,1)S(1)} collective-permute-done((bf16[128,2304]{1,0:T(8,128)(2,1)}, bf16[128,2304]{1,0:T(8,128)(2,1)S(1)}, u32[]{:S(2)}, u32[]{:S(2)}) %collective-permute-start.72) | collective-permute-done | bytes 589856 | tf_op jit(solution)/shard_map/ppermute | solution.py:65
  437.4 10.8 %collective-permute-done.73 = bf16[128,2304]{1,0:T(8,128)(2,1)S(1)} collective-permute-done((bf16[128,2304]{1,0:T(8,128)(2,1)S(1)}, bf16[128,2304]{1,0:T(8,128)(2,1)S(1)}, u32[]{:S(2)}, u32[]{:S(2)}) %collective-permute-start.73) | collective-permute-done | bytes 589856 | tf_op jit(solution)/shard_map/ppermute | solution.py:65
  464.3 9.9 %collective-permute-done.77 = bf16[128,2304]{1,0:T(8,128)(2,1)S(1)} collective-permute-done((bf16[128,2304]{1,0:T(8,128)(2,1)S(1)}, bf16[128,2304]{1,0:T(8,128)(2,1)S(1)}, u32[]{:S(2)}, u32[]{:S(2)}) %collective-permute-start.77) | collective-permute-done | bytes 589856 | tf_op jit(solution)/shard_map/ppermute | solution.py:65
  486.9 6.7 convolution_convert_fusion.1
  493.7 10.1 %convolution_convert_fusion.2 = bf16[2304,1152]{1,0:T(8,128)(2,1)S(1)} fusion(bf16[1024,2304]{1,0:T(8,128)(2,1)} %get-tuple-element.115, bf16[256,1152]{1,0:T(8,128)(2,1)S(1)} %get-tuple-element.81, bf16[256,1152]{1,0:T(8,128)(2,1)S(1)} %get-tuple-element.79, bf16[256,1152]{1,0:T(8,128)(2,1)S(1)} %get-tuple-element.77, ...), kind=kOutput, calls=%fused_computation.3 | convolution fusion | flops 5447909376 | bytes 12386304 | tf_op jit(solution)/shard_map/dot_general | solution.py:43
  506.0 8.2 convolution_convert_fusion
  526.6 9.1 %collective-permute-done.85 = bf16[128,2304]{1,0:T(8,128)(2,1)S(1)} collective-permute-done((bf16[128,2304]{1,0:T(8,128)(2,1)S(1)}, bf16[128,2304]{1,0:T(8,128)(2,1)S(1)}, u32[]{:S(2)}, u32[]{:S(2)}) %collective-permute-start.85) | collective-permute-done | bytes 589856 | tf_op jit(solution)/shard_map/ppermute | solution.py:65
  535.8 11.7 %collective-permute-done.86 = bf16[128,2304]{1,0:T(8,128)(2,1)S(1)} collective-permute-done((bf16[128,2304]{1,0:T(8,128)(2,1)S(1)}, bf16[128,2304]{1,0:T(8,128)(2,1)S(1)}, u32[]{:S(2)}, u32[]{:S(2)}) %collective-permute-start.86) | collective-permute-done | bytes 589856 | tf_op jit(solution)/shard_map/ppermute | solution.py:65
  592.9 9.0 %collective-permute-done.89 = bf16[128,2304]{1,0:T(8,128)(2,1)S(1)} collective-permute-done((bf16[128,2304]{1,0:T(8,128)(2,1)S(1)}, bf16[128,2304]{1,0:T(8,128)(2,1)S(1)}, u32[]{:S(2)}, u32[]{:S(2)}) %collective-permute-start.89) | collective-permute-done | bytes 589856 | tf_op jit(solution)/shard_map/ppermute | solution.py:65
  649.6 13.8 %collective-permute-done.96 = bf16[288,512]{1,0:T(8,128)(2,1)S(1)} collective-permute-done((bf16[288,512]{1,0:T(8,128)(2,1)S(1)}, bf16[288,512]{1,0:T(8,128)(2,1)S(1)}, u32[]{:S(2)}, u32[]{:S(2)}) %collective-permute-start.96) | collective-permute-done | bytes 294944 | tf_op jit(solution)/shard_map/ppermute | solution.py:65
  663.7 11.4 %collective-permute-done.92 = bf16[288,512]{1,0:T(8,128)(2,1)S(1)} collective-permute-done((bf16[288,512]{1,0:T(8,128)(2,1)S(1)}, bf16[288,512]{1,0:T(8,128)(2,1)S(1)}, u32[]{:S(2)}, u32[]{:S(2)}) %collective-permute-start.92) | collective-permute-done | bytes 294944 | tf_op jit(solution)/shard_map/ppermute | solution.py:65
  716.7 18.0 %collective-permute-done.107 = bf16[4,288,576]{2,1,0:T(8,128)(2,1)S(1)} collective-permute-done((bf16[4,288,576]{2,1,0:T(8,128)(2,1)S(1)}, bf16[4,288,576]{2,1,0:T(8,128)(2,1)S(1)}, u32[]{:S(2)}, u32[]{:S(2)}) %collective-permute-start.107) | collective-permute-done | bytes 1327136 | tf_op jit(solution)/shard_map/ppermute | solution.py:65
  766.1 9.3 %collective-permute-start.109 = (bf16[288,576]{1,0:T(8,128)(2,1)}, bf16[288,576]{1,0:T(8,128)(2,1)}, u32[]{:S(2)}, u32[]{:S(2)}) collective-permute-start(bf16[288,576]{1,0:T(8,128)(2,1)} %get-tuple-element.97), channel_id=1, source_target_pairs={{0,16},{1,17},{2,18},{3,19},{4,20},{5,21},{6,22},{7,23},{8,24},{9,... | collective-permute-start | bytes 995336 | tf_op jit(solution)/shard_map/ppermute | solution.py:65
  787.9 9.9 %collective-permute-done.114 = bf16[288,576]{1,0:T(8,128)(2,1)} collective-permute-done((bf16[288,576]{1,0:T(8,128)(2,1)}, bf16[288,576]{1,0:T(8,128)(2,1)}, u32[]{:S(2)}, u32[]{:S(2)}) %collective-permute-start.114) | collective-permute-done | bytes 331808 | tf_op jit(solution)/shard_map/ppermute | solution.py:65
  816.7 14.2 %dynamic_update_slice.241 = bf16[4,288,576]{2,0,1:T(4,128)(2,1)} dynamic-update-slice(bf16[4,288,576]{2,0,1:T(4,128)(2,1)} %copy.96, bf16[1,288,576]{2,0,1:T(2,128)(2,1)S(1)} %copy.97, s32[]{:T(128)S(6)} %select_n.342, s32[]{:T(128)} %constant.285.clone.1, s32[]{:T(128)} %constant.285.clone.1) | dynamic-update-slice | bytes 663556 | tf_op jit(solution)/shard_map/dynamic_update_slice | solution.py:101
  830.9 14.2 %dynamic_update_slice.242 = bf16[4,288,576]{2,0,1:T(4,128)(2,1)} dynamic-update-slice(bf16[4,288,576]{2,0,1:T(4,128)(2,1)} %dynamic_update_slice.241, bf16[1,288,576]{2,0,1:T(2,128)(2,1)S(1)} %copy.98, s32[]{:T(128)S(6)} %select_n.344, s32[]{:T(128)} %constant.285.clone.1, s32[]{:T(128)} %constant.285.clone.1) | dynamic-update-slice | bytes 663556 | tf_op jit(solution)/shard_map/dynamic_update_slice | solution.py:101
  845.1 14.2 %dynamic_update_slice.243 = bf16[4,288,576]{2,0,1:T(4,128)(2,1)} dynamic-update-slice(bf16[4,288,576]{2,0,1:T(4,128)(2,1)} %dynamic_update_slice.242, bf16[1,288,576]{2,0,1:T(2,128)(2,1)S(1)} %copy.99, s32[]{:T(128)S(6)} %select_n.346, s32[]{:T(128)} %constant.285.clone.1, s32[]{:T(128)} %constant.285.clone.1) | dynamic-update-slice | bytes 663556 | tf_op jit(solution)/shard_map/dynamic_update_slice | solution.py:101
  (686 shorter events, 501.5 us)
Async XLA Ops:
  3.6 35.2 %collective-permute-start.7 = (bf16[288,1024]{1,0:T(8,128)(2,1)}, bf16[288,1024]{1,0:T(8,128)(2,1)}, u32[]{:S(2)}, u32[]{:S(2)}) collective-permute-start(bf16[288,1024]{1,0:T(8,128)(2,1)} %pad_maximum_fusion.17), channel_id=1, source_target_pairs={{0,4},{1,5},{2,6},{3,7},{4,0},{5,1},{6,2},{7,3},{8,12},{9,13},{10,... | collective-permute-start | bytes 1769480 | tf_op jit(solution)/shard_map/ppermute | solution.py:65
  33.6 59.3 %collective-permute-start.4 = (bf16[128,2304]{1,0:T(8,128)(2,1)}, bf16[128,2304]{1,0:T(8,128)(2,1)}, u32[]{:S(2)}, u32[]{:S(2)}) collective-permute-start(bf16[128,2304]{1,0:T(8,128)(2,1)} %fusion.100), channel_id=1, source_target_pairs={{0,1},{1,0},{2,3},{3,2},{4,5},{5,4},{6,7},{7,6},{8,9},{9,8},{10,11... | collective-permute-start | bytes 1769480 | tf_op jit(solution)/shard_map/ppermute | solution.py:65
  35.1 57.8 %collective-permute-start.5 = (bf16[128,2304]{1,0:T(8,128)(2,1)}, bf16[128,2304]{1,0:T(8,128)(2,1)}, u32[]{:S(2)}, u32[]{:S(2)}) collective-permute-start(bf16[128,2304]{1,0:T(8,128)(2,1)} %fusion.100), channel_id=1, source_target_pairs={{0,2},{1,3},{2,0},{3,1},{4,6},{5,7},{6,4},{7,5},{8,10},{9,11},{10,... | collective-permute-start | bytes 1769480 | tf_op jit(solution)/shard_map/ppermute | solution.py:65
  89.4 30.9 %collective-permute-start.18 = (bf16[288,512]{1,0:T(8,128)(2,1)}, bf16[288,512]{1,0:T(8,128)(2,1)}, u32[]{:S(2)}, u32[]{:S(2)}) collective-permute-start(bf16[288,512]{1,0:T(8,128)(2,1)} %collective-permute-done.17), channel_id=1, source_target_pairs={{0,4},{1,5},{2,6},{3,7},{4,0},{5,1},{6,2},{7,3},{8,12},{9,13},{10,... | collective-permute-start | bytes 884744 | tf_op jit(solution)/shard_map/ppermute | solution.py:65
  135.4 31.8 %collective-permute-start.23 = (bf16[128,2304]{1,0:T(8,128)(2,1)S(1)}, bf16[128,2304]{1,0:T(8,128)(2,1)S(1)}, u32[]{:S(2)}, u32[]{:S(2)}) collective-permute-start(bf16[128,2304]{1,0:T(8,128)(2,1)S(1)} %get-tuple-element.86), channel_id=1, source_target_pairs={{0,3},{1,2},{2,1},{3,0},{4,7},{5,6},{6,5},{7,4},{8,11},{9,10},{10,... | collective-permute-start | bytes 1769480 | tf_op jit(solution)/shard_map/ppermute | solution.py:65
  137.4 32.0 %collective-permute-start.28 = (bf16[288,576]{1,0:T(8,128)(2,1)S(1)}, bf16[288,576]{1,0:T(8,128)(2,1)S(1)}, u32[]{:S(2)}, u32[]{:S(2)}) collective-permute-start(bf16[288,576]{1,0:T(8,128)(2,1)S(1)} %bitcast.495), channel_id=1, source_target_pairs={{0,8},{1,9},{2,10},{3,11},{4,12},{5,13},{6,14},{7,15},{8,16},{9,17... | collective-permute-start | bytes 995336 | tf_op jit(solution)/shard_map/ppermute | solution.py:65
  142.4 87.8 %collective-permute-start.31 = (bf16[288,576]{1,0:T(8,128)(2,1)S(1)}, bf16[288,576]{1,0:T(8,128)(2,1)S(1)}, u32[]{:S(2)}, u32[]{:S(2)}) collective-permute-start(bf16[288,576]{1,0:T(8,128)(2,1)S(1)} %bitcast.493), channel_id=1, source_target_pairs={{0,16},{1,17},{2,18},{3,19},{4,20},{5,21},{6,22},{7,23},{8,24},{9,... | collective-permute-start | bytes 995336 | tf_op jit(solution)/shard_map/ppermute | solution.py:65
  169.4 62.1 %collective-permute-start.34 = (bf16[288,576]{1,0:T(8,128)(2,1)S(1)}, bf16[288,576]{1,0:T(8,128)(2,1)S(1)}, u32[]{:S(2)}, u32[]{:S(2)}) collective-permute-start(bf16[288,576]{1,0:T(8,128)(2,1)S(1)} %bitcast.490), channel_id=1, source_target_pairs={{0,24},{1,25},{2,26},{3,27},{4,28},{5,29},{6,30},{7,31},{8,0},{9,1... | collective-permute-start | bytes 995336 | tf_op jit(solution)/shard_map/ppermute | solution.py:65
  194.1 38.9 %collective-permute-start.42 = (bf16[288,576]{1,0:T(8,128)(2,1)S(1)}, bf16[288,576]{1,0:T(8,128)(2,1)S(1)}, u32[]{:S(2)}, u32[]{:S(2)}) collective-permute-start(bf16[288,576]{1,0:T(8,128)(2,1)S(1)} %bitcast.492), channel_id=1, source_target_pairs={{0,16},{1,17},{2,18},{3,19},{4,20},{5,21},{6,22},{7,23},{8,24},{9,... | collective-permute-start | bytes 995336 | tf_op jit(solution)/shard_map/ppermute | solution.py:65
  223.0 35.7 %collective-permute-start.45 = (bf16[288,576]{1,0:T(8,128)(2,1)S(1)}, bf16[288,576]{1,0:T(8,128)(2,1)S(1)}, u32[]{:S(2)}, u32[]{:S(2)}) collective-permute-start(bf16[288,576]{1,0:T(8,128)(2,1)S(1)} %bitcast.488), channel_id=1, source_target_pairs={{0,24},{1,25},{2,26},{3,27},{4,28},{5,29},{6,30},{7,31},{8,0},{9,1... | collective-permute-start | bytes 995336 | tf_op jit(solution)/shard_map/ppermute | solution.py:65
  231.5 27.9 %collective-permute-start.56 = (bf16[288,576]{1,0:T(8,128)(2,1)S(1)}, bf16[288,576]{1,0:T(8,128)(2,1)S(1)}, u32[]{:S(2)}, u32[]{:S(2)}) collective-permute-start(bf16[288,576]{1,0:T(8,128)(2,1)S(1)} %bitcast.489), channel_id=1, source_target_pairs={{0,24},{1,25},{2,26},{3,27},{4,28},{5,29},{6,30},{7,31},{8,0},{9,1... | collective-permute-start | bytes 995336 | tf_op jit(solution)/shard_map/ppermute | solution.py:65
  258.8 33.3 %collective-permute-start.35 = (bf16[288,576]{1,0:T(8,128)(2,1)S(1)}, bf16[288,576]{1,0:T(8,128)(2,1)S(1)}, u32[]{:S(2)}, u32[]{:S(2)}) collective-permute-start(bf16[288,576]{1,0:T(8,128)(2,1)S(1)} %collective-permute-done.34), channel_id=1, source_target_pairs={{0,1},{1,0},{2,3},{3,2},{4,5},{5,4},{6,7},{7,6},{8,9},{9,8},{10,11... | collective-permute-start | bytes 995336 | tf_op jit(solution)/shard_map/ppermute | solution.py:65
  259.4 33.2 %collective-permute-start.46 = (bf16[288,576]{1,0:T(8,128)(2,1)S(1)}, bf16[288,576]{1,0:T(8,128)(2,1)S(1)}, u32[]{:S(2)}, u32[]{:S(2)}) collective-permute-start(bf16[288,576]{1,0:T(8,128)(2,1)S(1)} %collective-permute-done.45), channel_id=1, source_target_pairs={{0,1},{1,0},{2,3},{3,2},{4,5},{5,4},{6,7},{7,6},{8,9},{9,8},{10,11... | collective-permute-start | bytes 995336 | tf_op jit(solution)/shard_map/ppermute | solution.py:65
  260.9 32.7 %collective-permute-start.57 = (bf16[288,576]{1,0:T(8,128)(2,1)S(1)}, bf16[288,576]{1,0:T(8,128)(2,1)S(1)}, u32[]{:S(2)}, u32[]{:S(2)}) collective-permute-start(bf16[288,576]{1,0:T(8,128)(2,1)S(1)} %collective-permute-done.56), channel_id=1, source_target_pairs={{0,1},{1,0},{2,3},{3,2},{4,5},{5,4},{6,7},{7,6},{8,9},{9,8},{10,11... | collective-permute-start | bytes 995336 | tf_op jit(solution)/shard_map/ppermute | solution.py:65
  404.5 111.6 %collective-permute-start.84 = (bf16[128,2304]{1,0:T(8,128)(2,1)S(1)}, bf16[128,2304]{1,0:T(8,128)(2,1)S(1)}, u32[]{:S(2)}, u32[]{:S(2)}) collective-permute-start(bf16[128,2304]{1,0:T(8,128)(2,1)S(1)} %slice.317), channel_id=1, source_target_pairs={{0,2},{1,3},{2,0},{3,1},{4,6},{5,7},{6,4},{7,5},{8,10},{9,11},{10,... | collective-permute-start | bytes 1769480 | tf_op jit(solution)/shard_map/ppermute | solution.py:65
  406.6 28.0 %collective-permute-start.75 = (bf16[128,2304]{1,0:T(8,128)(2,1)}, bf16[128,2304]{1,0:T(8,128)(2,1)S(1)}, u32[]{:S(2)}, u32[]{:S(2)}) collective-permute-start(bf16[128,2304]{1,0:T(8,128)(2,1)} %collective-permute-done.71), channel_id=1, source_target_pairs={{0,8},{1,9},{2,10},{3,11},{4,12},{5,13},{6,14},{7,15},{8,16},{9,17... | collective-permute-start | bytes 1769480 | tf_op jit(solution)/shard_map/ppermute | solution.py:65
  474.4 29.5 %collective-permute-start.78 = (bf16[128,2304]{1,0:T(8,128)(2,1)S(1)}, bf16[128,2304]{1,0:T(8,128)(2,1)S(1)}, u32[]{:S(2)}, u32[]{:S(2)}) collective-permute-start(bf16[128,2304]{1,0:T(8,128)(2,1)S(1)} %fusion.118), channel_id=1, source_target_pairs={{0,8},{1,9},{2,10},{3,11},{4,12},{5,13},{6,14},{7,15},{8,16},{9,17... | collective-permute-start | bytes 1769480 | tf_op jit(solution)/shard_map/ppermute | solution.py:65
  516.2 115.8 %collective-permute-start.116 = (bf16[4,288,1152]{2,1,0:T(8,128)(2,1)}, bf16[4,288,1152]{2,1,0:T(8,128)(2,1)}, u32[]{:S(2)}, u32[]{:S(2)}) collective-permute-start(bf16[4,288,1152]{2,1,0:T(8,128)(2,1)} %dynamic-slice_bitcast_fusion), channel_id=1, source_target_pairs={{0,4},{1,5},{2,6},{3,7},{4,0},{5,1},{6,2},{7,3},{8,12},{9,13},{10,... | collective-permute-start | bytes 7962632 | tf_op jit(solution)/shard_map/ppermute | solution.py:65
  616.3 27.8 %collective-permute-start.102 = (bf16[4,288,512]{2,1,0:T(8,128)(2,1)}, bf16[4,288,512]{2,1,0:T(8,128)(2,1)}, u32[]{:S(2)}, u32[]{:S(2)}) collective-permute-start(bf16[4,288,512]{2,1,0:T(8,128)(2,1)} %dynamic-slice_bitcast_fusion.3), channel_id=1, source_target_pairs={{0,4},{1,5},{2,6},{3,7},{4,0},{5,1},{6,2},{7,3},{8,12},{9,13},{10,... | collective-permute-start | bytes 3538952 | tf_op jit(solution)/shard_map/ppermute | solution.py:65
  636.3 76.2 %collective-permute-start.117 = (bf16[4,288,576]{2,1,0:T(8,128)(2,1)S(1)}, bf16[4,288,576]{2,1,0:T(8,128)(2,1)S(1)}, u32[]{:S(2)}, u32[]{:S(2)}) collective-permute-start(bf16[4,288,576]{2,1,0:T(8,128)(2,1)S(1)} %slice.314), channel_id=1, source_target_pairs={{0,1},{1,0},{2,3},{3,2},{4,5},{5,4},{6,7},{7,6},{8,9},{9,8},{10,11... | collective-permute-start | bytes 3981320 | tf_op jit(solution)/shard_map/ppermute | solution.py:65
  640.1 75.1 %collective-permute-start.112 = (bf16[4,288,576]{2,1,0:T(8,128)(2,1)S(1)}, bf16[4,288,576]{2,1,0:T(8,128)(2,1)S(1)}, u32[]{:S(2)}, u32[]{:S(2)}) collective-permute-start(bf16[4,288,576]{2,1,0:T(8,128)(2,1)S(1)} %slice.315), channel_id=1, source_target_pairs={{0,1},{1,0},{2,3},{3,2},{4,5},{5,4},{6,7},{7,6},{8,9},{9,8},{10,11... | collective-permute-start | bytes 3981320 | tf_op jit(solution)/shard_map/ppermute | solution.py:65
  644.1 90.6 %collective-permute-start.107 = (bf16[4,288,576]{2,1,0:T(8,128)(2,1)S(1)}, bf16[4,288,576]{2,1,0:T(8,128)(2,1)S(1)}, u32[]{:S(2)}, u32[]{:S(2)}) collective-permute-start(bf16[4,288,576]{2,1,0:T(8,128)(2,1)S(1)} %slice.316), channel_id=1, source_target_pairs={{0,1},{1,0},{2,3},{3,2},{4,5},{5,4},{6,7},{7,6},{8,9},{9,8},{10,11... | collective-permute-start | bytes 3981320 | tf_op jit(solution)/shard_map/ppermute | solution.py:65
  706.7 34.4 %collective-permute-start.99 = (bf16[288,512]{1,0:T(8,128)(2,1)S(1)}, bf16[288,512]{1,0:T(8,128)(2,1)S(1)}, u32[]{:S(2)}, u32[]{:S(2)}) collective-permute-start(bf16[288,512]{1,0:T(8,128)(2,1)S(1)} %get-tuple-element.37), channel_id=1, source_target_pairs={{0,1},{1,0},{2,3},{3,2},{4,5},{5,4},{6,7},{7,6},{8,9},{9,8},{10,11... | collective-permute-start | bytes 884744 | tf_op jit(solution)/shard_map/ppermute | solution.py:65
  710.5 31.1 %collective-permute-start.100 = (bf16[288,512]{1,0:T(8,128)(2,1)S(1)}, bf16[288,512]{1,0:T(8,128)(2,1)S(1)}, u32[]{:S(2)}, u32[]{:S(2)}) collective-permute-start(bf16[288,512]{1,0:T(8,128)(2,1)S(1)} %get-tuple-element.37), channel_id=1, source_target_pairs={{0,2},{1,3},{2,0},{3,1},{4,6},{5,7},{6,4},{7,5},{8,10},{9,11},{10,... | collective-permute-start | bytes 884744 | tf_op jit(solution)/shard_map/ppermute | solution.py:65
  712.5 33.8 %collective-permute-start.101 = (bf16[288,512]{1,0:T(8,128)(2,1)S(1)}, bf16[288,512]{1,0:T(8,128)(2,1)S(1)}, u32[]{:S(2)}, u32[]{:S(2)}) collective-permute-start(bf16[288,512]{1,0:T(8,128)(2,1)S(1)} %get-tuple-element.37), channel_id=1, source_target_pairs={{0,3},{1,2},{2,1},{3,0},{4,7},{5,6},{6,5},{7,4},{8,11},{9,10},{10,... | collective-permute-start | bytes 884744 | tf_op jit(solution)/shard_map/ppermute | solution.py:65
  716.3 37.3 %collective-permute-start.118 = (bf16[288,576]{1,0:T(8,128)(2,1)}, bf16[288,576]{1,0:T(8,128)(2,1)}, u32[]{:S(2)}, u32[]{:S(2)}) collective-permute-start(bf16[288,576]{1,0:T(8,128)(2,1)} %get-tuple-element.90), channel_id=1, source_target_pairs={{0,8},{1,9},{2,10},{3,11},{4,12},{5,13},{6,14},{7,15},{8,16},{9,17... | collective-permute-start | bytes 995336 | tf_op jit(solution)/shard_map/ppermute | solution.py:65
  741.6 35.0 %collective-permute-start.113 = (bf16[288,576]{1,0:T(8,128)(2,1)}, bf16[288,576]{1,0:T(8,128)(2,1)}, u32[]{:S(2)}, u32[]{:S(2)}) collective-permute-start(bf16[288,576]{1,0:T(8,128)(2,1)} %get-tuple-element.94), channel_id=1, source_target_pairs={{0,8},{1,9},{2,10},{3,11},{4,12},{5,13},{6,14},{7,15},{8,16},{9,17... | collective-permute-start | bytes 995336 | tf_op jit(solution)/shard_map/ppermute | solution.py:65
  746.2 51.6 %collective-permute-start.114 = (bf16[288,576]{1,0:T(8,128)(2,1)}, bf16[288,576]{1,0:T(8,128)(2,1)}, u32[]{:S(2)}, u32[]{:S(2)}) collective-permute-start(bf16[288,576]{1,0:T(8,128)(2,1)} %get-tuple-element.93), channel_id=1, source_target_pairs={{0,16},{1,17},{2,18},{3,19},{4,20},{5,21},{6,22},{7,23},{8,24},{9,... | collective-permute-start | bytes 995336 | tf_op jit(solution)/shard_map/ppermute | solution.py:65
  753.6 45.9 %collective-permute-start.115 = (bf16[288,576]{1,0:T(8,128)(2,1)}, bf16[288,576]{1,0:T(8,128)(2,1)}, u32[]{:S(2)}, u32[]{:S(2)}) collective-permute-start(bf16[288,576]{1,0:T(8,128)(2,1)} %get-tuple-element.92), channel_id=1, source_target_pairs={{0,24},{1,25},{2,26},{3,27},{4,28},{5,29},{6,30},{7,31},{8,0},{9,1... | collective-permute-start | bytes 995336 | tf_op jit(solution)/shard_map/ppermute | solution.py:65
  755.2 52.5 %collective-permute-start.108 = (bf16[288,576]{1,0:T(8,128)(2,1)}, bf16[288,576]{1,0:T(8,128)(2,1)}, u32[]{:S(2)}, u32[]{:S(2)}) collective-permute-start(bf16[288,576]{1,0:T(8,128)(2,1)} %get-tuple-element.98), channel_id=1, source_target_pairs={{0,8},{1,9},{2,10},{3,11},{4,12},{5,13},{6,14},{7,15},{8,16},{9,17... | collective-permute-start | bytes 995336 | tf_op jit(solution)/shard_map/ppermute | solution.py:65
  766.1 47.5 %collective-permute-start.109 = (bf16[288,576]{1,0:T(8,128)(2,1)}, bf16[288,576]{1,0:T(8,128)(2,1)}, u32[]{:S(2)}, u32[]{:S(2)}) collective-permute-start(bf16[288,576]{1,0:T(8,128)(2,1)} %get-tuple-element.97), channel_id=1, source_target_pairs={{0,16},{1,17},{2,18},{3,19},{4,20},{5,21},{6,22},{7,23},{8,24},{9,... | collective-permute-start | bytes 995336 | tf_op jit(solution)/shard_map/ppermute | solution.py:65
  777.4 37.7 %collective-permute-start.110 = (bf16[288,576]{1,0:T(8,128)(2,1)S(1)}, bf16[288,576]{1,0:T(8,128)(2,1)}, u32[]{:S(2)}, u32[]{:S(2)}) collective-permute-start(bf16[288,576]{1,0:T(8,128)(2,1)S(1)} %copy-done.37), channel_id=1, source_target_pairs={{0,24},{1,25},{2,26},{3,27},{4,28},{5,29},{6,30},{7,31},{8,0},{9,1... | collective-permute-start | bytes 995336 | tf_op jit(solution)/shard_map/ppermute | solution.py:65
  (190 other events, 2388.3 us)
